TPU v7x, 32 devices: a whole 2x2x4 slice. The times are simulated.
32 devices in a mesh: seq: 8 (over z, x), head: 4 (over y, core).
Axes of the slice: x: 2, y: 2, z: 4, core: 2. Of those that a mesh axis runs over, the one named last changes fastest.
Arguments:
- queries: bfloat16 [6144, 8192], P('seq', 'head'), may hold values from -6 to 6
- key_rows: bfloat16 [6144, 8192], P('seq', 'head'), may hold values from -0.5 to 0.5
- value_rows: bfloat16 [6144, 8192], P('seq', 'head'), may hold values from -130 to 130
- log_decay: float32 [64, 6144], P('head', 'seq'), may hold values from -1 to 0
- norm_gain: float32 [8192], P('head'), may hold values from 0.1 to 1.9
- grad_out: bfloat16 [6144, 8192], P('seq', 'head'), may hold values from -13 to 13
Outputs:
- output: bfloat16 [6144, 8192], P('seq', 'head')
- grad_queries: bfloat16 [6144, 8192], P('seq', 'head')
- grad_keys: bfloat16 [6144, 8192], P('seq', 'head')
- grad_values: bfloat16 [6144, 8192], P('seq', 'head')
- grad_gain: float32 [8192], P('head')
All inputs are finite; a program needn't handle non-finite values.
Results may differ from a plain program's by a relative error of at most 0.01.
Values sent between devices are 32-bit elements; how exact they have to be, the bound alone decides.
A program may use at most 192 MiB of HBM per device.

v0:
```python
import jax
import jax.numpy as jnp
from jax import lax
from jax.sharding import PartitionSpec as P

DH = 128
HD = 8192
EPSILON = 1e-06


def prefix(part, axis, combine, identity, reverse):
    count = lax.axis_size(axis)
    place = lax.axis_index(axis)
    ahead = count - 1 - place if reverse else place
    gathered = jax.tree.map(lambda a: lax.all_gather(a, axis), part)
    state = jax.tree.map(lambda a, e: jnp.zeros_like(a) + jnp.asarray(e, a.dtype), part, identity)

    def one(step, state):
        source = count - 1 - step if reverse else step
        return combine(
            state, jax.tree.map(lambda a: lax.dynamic_index_in_dim(a, source, 0, False), gathered)
        )

    return lax.fori_loop(0, ahead, one, state)


def split_pair(operand):
    high = operand.astype(jnp.bfloat16)
    low = (operand - high.astype(jnp.float32)).astype(jnp.bfloat16)
    return (high, low)


def split_product(form, left, right):
    if left.dtype == jnp.float32:
        high, low = split_pair(left)
        return jnp.einsum(form, high, right, preferred_element_type=jnp.float32) + jnp.einsum(
            form, low, right, preferred_element_type=jnp.float32
        )
    if right.dtype == jnp.float32:
        high, low = split_pair(right)
        return jnp.einsum(form, left, high, preferred_element_type=jnp.float32) + jnp.einsum(
            form, left, low, preferred_element_type=jnp.float32
        )
    return jnp.einsum(form, left, right, preferred_element_type=jnp.float32)


def causal_decay(cumulative):
    length = cumulative.shape[-1]
    below_diag = jnp.arange(length)[:, None] >= jnp.arange(length)[None, :]
    spread = cumulative[..., :, None] - cumulative[..., None, :]
    return jnp.where(below_diag, jnp.exp(jnp.where(below_diag, spread, 0.0)), 0.0)


def split_heads(matrix):
    return matrix.reshape(matrix.shape[0], -1, DH).transpose(1, 0, 2)


def merge_heads(tensor):
    return tensor.transpose(1, 0, 2).reshape(tensor.shape[1], -1)


def affine_combine(earlier, later):
    return (earlier[0] * later[0], later[0][:, None, None] * earlier[1] + later[1])


def intra_forward(operands):
    q_head, k_head, v_head, cumul = operands
    decay_mask = causal_decay(cumul)
    scores = jnp.dot(q_head, k_head.T, preferred_element_type=jnp.float32)
    weights = (scores * decay_mask).astype(jnp.bfloat16)
    return jnp.dot(weights, v_head, preferred_element_type=jnp.float32)


def intra_backward(operands):
    q_head, k_head, v_head, grad_head, cumul = operands
    decay_mask = causal_decay(cumul)
    scores = jnp.dot(q_head, k_head.T, preferred_element_type=jnp.float32)
    weights = (scores * decay_mask).astype(jnp.bfloat16)
    grad_scores = jnp.dot(grad_head, v_head.T, preferred_element_type=jnp.float32)
    grad_weights = (grad_scores * decay_mask).astype(jnp.bfloat16)
    grad_q = jnp.dot(grad_weights, k_head, preferred_element_type=jnp.float32)
    grad_k = jnp.dot(grad_weights.T, q_head, preferred_element_type=jnp.float32)
    grad_v = jnp.dot(weights.T, grad_head, preferred_element_type=jnp.float32)
    return (grad_q, grad_k, grad_v)


def on_device(queries, key_rows, value_rows, log_decay, norm_gain, grad_out):
    q_heads = split_heads(queries)
    k_heads = split_heads(key_rows)
    v_heads = split_heads(value_rows)
    cumulative = jnp.cumsum(log_decay, axis=1)
    block_total = cumulative[:, -1]
    growth = jnp.exp(cumulative)[..., None]
    tail = jnp.exp(block_total[:, None] - cumulative)[..., None]
    decay_total = jnp.exp(block_total)
    local_state = split_product("htd,hte->hde", k_heads * tail, v_heads)
    identity = (jnp.ones_like(decay_total), jnp.zeros_like(local_state))
    state_in = prefix((decay_total, local_state), "seq", affine_combine, identity, False)[1]
    intra = lax.map(intra_forward, (q_heads, k_heads, v_heads, cumulative))
    attended = intra + growth * split_product("htd,hde->hte", q_heads, state_in)
    mixed = merge_heads(attended)
    scaled_grad = grad_out.astype(jnp.float32) * norm_gain[None, :]
    square_sum = lax.psum(jnp.sum(mixed * mixed, axis=1), "head")
    inverse = lax.rsqrt(square_sum / HD + EPSILON)
    normed = mixed * inverse[:, None]
    inner_sum = lax.psum(jnp.sum(scaled_grad * normed, axis=1), "head")
    center = inner_sum / HD
    output = (normed * norm_gain[None, :]).astype(jnp.bfloat16)
    gain_part = jnp.sum(grad_out.astype(jnp.float32) * normed, axis=0)
    grad_gain = lax.psum(gain_part, "seq")
    grad_mixed = (inverse[:, None] * (scaled_grad - normed * center[:, None])).astype(jnp.bfloat16)
    grad_heads = split_heads(grad_mixed)
    state_grad = split_product("htd,hte->hde", q_heads * growth, grad_heads)
    identity = (jnp.ones_like(decay_total), jnp.zeros_like(state_grad))
    state_after = prefix((decay_total, state_grad), "seq", affine_combine, identity, True)[1]
    intra_q, intra_k, intra_v = lax.map(
        intra_backward, (q_heads, k_heads, v_heads, grad_heads, cumulative)
    )
    grad_q = intra_q + growth * split_product("hte,hde->htd", grad_heads, state_in)
    grad_k = intra_k + tail * split_product("hse,hde->hsd", v_heads, state_after)
    grad_v = intra_v + tail * split_product("hsd,hde->hse", k_heads, state_after)
    return (
        output,
        merge_heads(grad_q).astype(jnp.bfloat16),
        merge_heads(grad_k).astype(jnp.bfloat16),
        merge_heads(grad_v).astype(jnp.bfloat16),
        grad_gain,
    )


def solution(mesh):
    in_specs = (
        P("seq", "head"),
        P("seq", "head"),
        P("seq", "head"),
        P("head", "seq"),
        P("head"),
        P("seq", "head"),
    )
    out_specs = (P("seq", "head"), P("seq", "head"), P("seq", "head"), P("seq", "head"), P("head"))
    return jax.shard_map(
        on_device, mesh=mesh, in_specs=in_specs, out_specs=out_specs, check_vma=False
    )
```

profile of v0, /device:TPU:0, one launch (start us, length us, event | category | flops | bytes accessed | tf_op | source)
XLA Modules:
  0.0 436.8 jit_solution(12516096848934879581)
XLA Ops:
  7.2 3.2 copy.65
  12.4 4.7 %copy.68 = bf16[768,2048]{0,1:T(8,128)(2,1)} copy(bf16[768,2048]{1,0:T(8,128)(2,1)} %param.16) | data formatting | bytes 6291456 | tf_op args[2]
  17.4 3.0 fusion.62
  25.3 4.6 %copy.71 = bf16[16,768,128]{2,1,0:T(8,128)(2,1)} copy(bf16[16,768,128]{1,2,0:T(8,128)(2,1)} %bitcast.184) | data formatting | bytes 6291456 | tf_op jit(solution)/shard_map/while | solution.py:99
  29.9 3.3 copy.64
  33.3 3.3 copy.69
  38.1 24.4 %all-reduce = f32[128]{0:T(128)S(1)} all-reduce(f32[128]{0:T(128)S(1)} %dynamic-update-slice), channel_id=2, replica_groups=mesh['seq'=8,'head'=4] {'seq'}, use_global_device_ids=true, to_apply=%add | all-reduce | flops 128 | bytes 1024
  62.6 3.4 broadcast.34.clone2
  65.9 45.5 %while.50 = (s32[]{:T(128)}, f32[16,768,128]{1,2,0:T(8,128)}, bf16[16,768,128]{2,1,0:T(8,128)(2,1)}, bf16[16,768,128]{2,1,0:T(8,128)(2,1)}, f32[16,768]{1,0:T(8,...) while((s32[]{:T(128)}, f32[16,768,128]{1,2,0:T(8,128)}, bf16[16,768,128]{2,1,0:T(8,128)(2,1)}, ...), condition=%wide.region_3.4_spmd, body=%wide.region_2.3_spmd.sunk | while | flops 305528832 | bytes 999513 | solution.py:99
  111.4 38.8 %all-gather.6.cloned.1.call-done = f32[128,128,128]{2,1,0:T(8,128)} async-done(((f32[16,128,128]{2,1,0:T(8,128)}), f32[128,128,128]{2,1,0:T(8,128)}) %all-gather.6.cloned.1.call-update) | async-done | bytes 8388624 | tf_op jit(solution)/shard_map/all_gather | solution.py:15
  150.3 3.1 fusion.81
  155.0 4.4 fusion.59
  159.4 6.6 %copy.79 = f32[768,2048]{1,0:T(8,128)} copy(f32[768,2048]{0,1:T(8,128)} %bitcast.193) | data formatting | bytes 12582912 | tf_op jit(solution)/shard_map/reshape | solution.py:59
  165.9 5.8 %psum.21 = f32[768]{0:T(1024)S(1)} all-reduce(f32[768]{0:T(1024)S(1)} %get-tuple-element.338), channel_id=1, replica_groups=mesh['seq'=8,'head'=4] {'head'}, use_global_device_ids=true, to_apply=%region_7.8 | all-reduce | flops 768 | bytes 6144 | tf_op jit(solution)/shard_map/psum | solution.py:103
  171.8 4.8 %fusion.56 = (f32[2048]{0:T(1024)S(1)}, f32[768]{0:T(1024)S(1)}) fusion(bf16[768,2048]{1,0:T(8,128)(2,1)} %param.19, f32[768,2048]{1,0:T(8,128)} %copy.79, f32[768]{0:T(1024)S(1)} %add_rsqrt_fusion, f32[2048]{0:T(1024)S(1)} %copy-done.11), kind=kLoop, calls=%fused_computation.62 | loop fusion | flops 11007232 | bytes 9459712 | tf_op jit(solution)/shard_map/reduce_sum | solution.py:109
  176.6 6.4 %psum.22 = f32[768]{0:T(1024)S(1)} all-reduce(f32[768]{0:T(1024)S(1)} %get-tuple-element.281), channel_id=1, replica_groups=mesh['seq'=8,'head'=4] {'head'}, use_global_device_ids=true, to_apply=%region_9.10 | all-reduce | flops 768 | bytes 6144 | tf_op jit(solution)/shard_map/psum | solution.py:106
  183.0 5.9 %fusion.68 = (bf16[96,16,8,128]{3,2,1,0:T(8,128)(2,1)S(1)}, bf16[768,2048]{1,0:T(8,128)(2,1)}) fusion(f32[768,2048]{1,0:T(8,128)} %copy.79, bf16[768,2048]{1,0:T(8,128)(2,1)} %param.19, f32[768]{0:T(1024)S(1)} %broadcast_multiply_fusion, f32[2048]{0:T(1024)S(1)} %copy-done.11, f32[768]{0:T(1024)S(1)} %add_rsqrt_fusion), kind=kLoop, calls=%fused_computation.82 | loop fusion | flops 14155776 | bytes 15742976
  191.5 3.7 fusion.79
  198.6 3.2 broadcast.34.clone
  201.8 3.3 broadcast.34.clone2.1
  205.1 3.2 broadcast.34.clone2.2
  208.3 137.7 %while.52 = (s32[]{:T(128)}, f32[16,768,128]{1,2,0:T(8,128)}, f32[16,768,128]{1,2,0:T(8,128)}, f32[16,768,128]{1,2,0:T(8,128)}, bf16[16,768,128]{2,1,0:T(8,128)(...) while((s32[]{:T(128)}, f32[16,768,128]{1,2,0:T(8,128)}, ...), condition=%wide.region_11.12_spmd, body=%wide.region_10.11_spmd.sunk | while | flops 762052608 | bytes 6122609 | solution.py:116
  346.1 8.5 %add_convert_fusion = bf16[16,768,128]{1,2,0:T(8,128)(2,1)} fusion(f32[16,768,128]{1,2,0:T(8,128)} %get-tuple-element.216, f32[16,768,128]{1,2,0:T(8,128)} %fusion.79, f32[16,768]{1,0:T(8,128)S(1)} %get-tuple-element.336, f32[16,128,128]{2,1,0:T(8,128)S(1)} %get-tuple-element.215, bf16[96,16,8,128]{3,2,1,0:T(8,128)(2,1)} %copy-done.9), kind=kOutput, calls=%fused_computation.73 | convolution fusion | flops 409993216 | bytes 19972096 | tf_op jit(solution)/shard_map/hte,hde->htd/dot_general | solution.py:41
  354.6 4.6 %copy.93 = bf16[768,2048]{1,0:T(8,128)(2,1)} copy(bf16[768,2048]{0,1:T(8,128)(2,1)} %bitcast.194) | data formatting | bytes 6291456
  359.2 30.1 %psum.23 = f32[2048]{0:T(1024)} all-reduce(f32[2048]{0:T(1024)S(1)} %get-tuple-element.280), channel_id=1, replica_groups=mesh['seq'=8,'head'=4] {'seq'}, use_global_device_ids=true, to_apply=%region_15.16 | all-reduce | flops 2048 | bytes 16384 | tf_op jit(solution)/shard_map/psum | solution.py:110
  389.4 10.7 %while.53 = (s32[]{:T(128)}, f32[16,128,128]{2,1,0:T(8,128)S(1)}, s32[]{:T(128)}, f32[8,16]{1,0:T(8,128)S(1)}, f32[8,16,128,128]{3,2,1,0:T(8,128)}, /*index=5*/s32[]{:T(128)}, s32[]{:T(128)}, s32[]{:T(128)}, s32[]{:T(128)}) while((s32[]{:T(128)}, f32[16,128,128]{2,1,0:T(8,128)S(1)}, s32[]{:T(128)}, f32[8,16]{1,0:T(8,128)S(1)}, ...), condition=%wide.region_13.14_spmd, body=%wide.region_12.13_spmd.sunk | while | flops 524294 | bytes 3146075 | solution.py:24
  400.1 3.0 fusion.77
  403.1 3.7 fusion.75
  406.8 5.5 %fusion.58 = bf16[16,768,128]{1,2,0:T(8,128)(2,1)} fusion(f32[16,768,128]{1,2,0:T(8,128)} %get-tuple-element.217, f32[16,128,768]{2,1,0:T(8,128)S(1)} %fusion.77, f32[16,768]{1,0:T(8,128)S(1)} %get-tuple-element.337, bf16[16,768,128]{1,2,0:T(8,128)(2,1)S(1)} %bitcast.187, f32[16,128,128]{2,1,0:T(8,128)S(1)} %get-tuple-element.218), kind=kOutput, calls=%fused_computation.66 | convolution fusion | flops 409993216 | bytes 19972096 | tf_op jit(solution)/shard_map/hse,hde->hsd/dot_general | solution.py:41
  412.4 4.6 %copy.94 = bf16[768,2048]{1,0:T(8,128)(2,1)} copy(bf16[768,2048]{0,1:T(8,128)(2,1)} %bitcast.196) | data formatting | bytes 6291456
  417.0 8.3 %fusion.57 = bf16[16,768,128]{1,2,0:T(8,128)(2,1)} fusion(f32[16,768,128]{1,2,0:T(8,128)} %get-tuple-element.219, f32[16,128,768]{2,1,0:T(8,128)} %fusion.75, f32[16,768]{1,0:T(8,128)S(1)} %get-tuple-element.337, bf16[16,768,128]{1,2,0:T(8,128)(2,1)} %bitcast.181, f32[16,128,128]{2,1,0:T(8,128)S(1)} %get-tuple-element.218), kind=kOutput, calls=%fused_computation.64 | convolution fusion | flops 409993216 | bytes 19972096 | tf_op jit(solution)/shard_map/hsd,hde->hse/dot_general | solution.py:41
  425.3 4.6 %copy.95 = bf16[768,2048]{1,0:T(8,128)(2,1)} copy(bf16[768,2048]{0,1:T(8,128)(2,1)} %bitcast.195) | data formatting | bytes 6291456
  (178 shorter events, 209.0 us)
Async XLA Ops:
  7.2 3.3 copy-start
  7.2 143.0 %all-gather.6.cloned.1.call-start = ((), (), s32[]{:S(2)}) async-start(), calls=%async_computation | async-start | bytes 9437184 | tf_op jit(solution)/shard_map/all_gather | solution.py:15
  10.4 12.1 %copy-start.2 = (bf16[768,2048]{0,1:T(8,128)(2,1)}, bf16[768,2048]{0,1:T(8,128)(2,1)S(1)}, u32[]{:S(2)}) copy-start(bf16[768,2048]{0,1:T(8,128)(2,1)S(1)} %copy.65) | copy-start | bytes 9437188
  17.4 3.0 copy-start.4
  22.5 366.9 %all-gather.8.cloned.1.call-start = ((), (), s32[]{:S(2)}) async-start(), calls=%async_computation.1 | async-start | bytes 9437184 | tf_op jit(solution)/shard_map/all_gather | solution.py:15
  33.2 3.3 copy-start.6
  33.2 3.3 copy-start.12
  150.3 3.1 copy-start.7
  150.3 4.7 %copy-start.10 = (f32[16,768,128]{1,2,0:T(8,128)S(1)}, f32[16,768,128]{1,2,0:T(8,128)}, u32[]{:S(2)}) copy-start(f32[16,768,128]{1,2,0:T(8,128)} %get-tuple-element.214) | copy-start | bytes 18874372
  159.4 12.4 %copy-start.11 = (f32[2048]{0:T(1024)S(1)}, f32[2048]{0:T(1024)}, u32[]{:S(2)}) copy-start(f32[2048]{0:T(1024)} %param.18) | copy-start | bytes 24580
  188.9 7.4 %copy-start.9 = (bf16[96,16,8,128]{3,2,1,0:T(8,128)(2,1)}, bf16[96,16,8,128]{3,2,1,0:T(8,128)(2,1)S(1)}, u32[]{:S(2)}) copy-start(bf16[96,16,8,128]{3,2,1,0:T(8,128)(2,1)S(1)} %get-tuple-element.334) | copy-start | bytes 9437188
  191.5 3.7 copy-start.8
  400.1 3.0 copy-start.3
  403.1 3.7 copy-start.5
  425.3 4.6 %copy-start.1 = (f32[16,768]{1,0:T(8,128)S(1)}, f32[16,768]{1,0:T(8,128)}, u32[]{:S(2)}) copy-start(f32[16,768]{1,0:T(8,128)} %param.17) | copy-start | bytes 147460
Sparse Core Ops, SparseCore 0:
  22.6 127.5 all-gather.5
  198.7 132.5 all-gather.7
where the time goes:
time: 440 us; the launch traced here: 437 us
  matrix products  231 us (52%)
  blocking collectives  66.8 us (15%)
  local copies, waits for them, and re-layouts  61.9 us (14%)
  waiting for transfers between devices  38.8 us (9%)
  other arithmetic  22.7 us (5%)
  between operations  14.9 us (3%)
    dot_general x16, matrix products, intra_forward(): return jnp.dot(weights, v_head, preferred_element_type=jnp.float32)  45.1 us
    dot_general x16, matrix products, intra_backward(): grad_v = jnp.dot(weights.T, grad_head, preferred_element_type=jnp.float32)  44.1 us
    all_gather x2, waiting for transfers between devices, prefix(): gathered = jax.tree.map(lambda a: lax.all_gather(a, axis), part)  38.8 us
    dot_general x16, matrix products, intra_backward(): grad_q = jnp.dot(grad_weights, k_head, preferred_element_type=jnp.float32)  35.8 us
    dot_general x16, matrix products, intra_backward(): grad_k = jnp.dot(grad_weights.T, q_head, preferred_element_type=jnp.float32)  32.9 us
    psum x1, blocking collectives, on_device(): grad_gain = lax.psum(gain_part, 'seq')  30.1 us
    unnamed x35, local copies, waits for them, and re-layouts  27.5 us
    dot_general x4, matrix products, split_product(): jnp.einsum(form, left, low, preferred_element_type=jnp.float32)  26.7 us
  transfers between devices with their start and end apart: 2, of which 1 were waited for; matrix products, arithmetic and copies ran while one was open for 51% of the time, Pallas kernels for 0%

commit v1 on v0

--- a/solution.py
+++ b/solution.py
@@ -107,7 +107,11 @@
     center = inner_sum / HD
     output = (normed * norm_gain[None, :]).astype(jnp.bfloat16)
     gain_part = jnp.sum(grad_out.astype(jnp.float32) * normed, axis=0)
-    grad_gain = lax.psum(gain_part, "seq")
+    grad_gain = gain_part
+    for hop in (1, 2, 4):
+        grad_gain = grad_gain + lax.ppermute(
+            grad_gain, "seq", [(dev, dev ^ hop) for dev in range(8)]
+        )
     grad_mixed = (inverse[:, None] * (scaled_grad - normed * center[:, None])).astype(jnp.bfloat16)
     grad_heads = split_heads(grad_mixed)
     state_grad = split_product("htd,hte->hde", q_heads * growth, grad_heads)

time: 440 us -> 419 us (0.952)
  blocking collectives: 66.8 us -> 36.7 us
  starting transfers between devices: 0.08 us -> 13.6 us
  matrix products: 231 us -> 225 us
    psum x1 -> x0, blocking collectives: 30.1 us -> none  [on_device(): grad_gain = lax.psum(gain_part, 'seq')]
    ppermute x0 -> x3, starting transfers between devices: none -> 13.6 us  [on_device(): lax.ppermute(grad_gain, 'seq', [(dev, dev ^ hop) for dev in range(8)])]
    dot_general x4, matrix products: 26.7 us -> 21.4 us  [split_product(): jnp.einsum(form, left, low, preferred_element_type=jnp.float32)]
    unnamed x35 -> x39, local copies, waits for them, and re-layouts: 27.5 us -> 29.3 us
  transfers between devices with their start and end apart: 2 -> 5, of which waited for: 1 -> 1; matrix products, arithmetic and copies ran while one was open for 51% -> 53% of each run, Pallas kernels for 0% -> 0%
where the time goes in v1:
time: 419 us; the launch traced here: 416 us
  matrix products  225 us (54%)
  local copies, waits for them, and re-layouts  63.5 us (15%)
  waiting for transfers between devices  38.9 us (9%)
  blocking collectives  36.7 us (9%)
  other arithmetic  23.3 us (6%)
  between operations  14.9 us (4%)
  starting transfers between devices  13.6 us (3%)
    dot_general x16, matrix products, intra_forward(): return jnp.dot(weights, v_head, preferred_element_type=jnp.float32)  45.1 us
    dot_general x16, matrix products, intra_backward(): grad_v = jnp.dot(weights.T, grad_head, preferred_element_type=jnp.float32)  43.9 us
    all_gather x2, waiting for transfers between devices, prefix(): gathered = jax.tree.map(lambda a: lax.all_gather(a, axis), part)  38.9 us
    dot_general x16, matrix products, intra_backward(): grad_q = jnp.dot(grad_weights, k_head, preferred_element_type=jnp.float32)  36 us
    dot_general x16, matrix products, intra_backward(): grad_k = jnp.dot(grad_weights.T, q_head, preferred_element_type=jnp.float32)  32.9 us
    unnamed x39, local copies, waits for them, and re-layouts  29.3 us
    dot_general x16, matrix products, intra_backward(): jnp.dot(grad_head, v_head.T, preferred_element_type=jnp.float32)  24.5 us
    unnamed x1, blocking collectives  24.4 us
  transfers between devices with their start and end apart: 5, of which 1 were waited for; matrix products, arithmetic and copies ran while one was open for 53% of the time, Pallas kernels for 0%

profile of v1, /device:TPU:0, one launch (start us, length us, event | category | flops | bytes accessed | tf_op | source)
XLA Modules:
  0.0 416.4 jit_solution(17420622956230175730)
XLA Ops:
  7.2 3.2 copy.65
  12.4 4.7 %copy.68 = bf16[768,2048]{0,1:T(8,128)(2,1)} copy(bf16[768,2048]{1,0:T(8,128)(2,1)} %param.16) | data formatting | bytes 6291456 | tf_op args[2]
  17.4 3.0 fusion.62
  25.3 4.6 %copy.71 = bf16[16,768,128]{2,1,0:T(8,128)(2,1)} copy(bf16[16,768,128]{1,2,0:T(8,128)(2,1)} %bitcast.184) | data formatting | bytes 6291456 | tf_op jit(solution)/shard_map/while | solution.py:99
  30.0 3.3 copy.64
  33.3 3.2 copy.69
  37.9 24.4 %all-reduce = f32[128]{0:T(128)S(1)} all-reduce(f32[128]{0:T(128)S(1)} %dynamic-update-slice), channel_id=2, replica_groups=mesh['seq'=8,'head'=4] {'seq'}, use_global_device_ids=true, to_apply=%add | all-reduce | flops 128 | bytes 1024
  62.5 3.4 broadcast.34.clone2
  65.8 45.5 %while.50 = (s32[]{:T(128)}, f32[16,768,128]{1,2,0:T(8,128)}, bf16[16,768,128]{2,1,0:T(8,128)(2,1)}, bf16[16,768,128]{2,1,0:T(8,128)(2,1)}, f32[16,768]{1,0:T(8,...) while((s32[]{:T(128)}, f32[16,768,128]{1,2,0:T(8,128)}, bf16[16,768,128]{2,1,0:T(8,128)(2,1)}, ...), condition=%wide.region_3.4_spmd, body=%wide.region_2.3_spmd.sunk | while | flops 305528832 | bytes 999513 | solution.py:99
  111.3 38.9 %all-gather.6.cloned.1.call-done = f32[128,128,128]{2,1,0:T(8,128)} async-done(((f32[16,128,128]{2,1,0:T(8,128)}), f32[128,128,128]{2,1,0:T(8,128)}) %all-gather.6.cloned.1.call-update) | async-done | bytes 8388624 | tf_op jit(solution)/shard_map/all_gather | solution.py:15
  150.4 3.1 fusion.81
  155.0 4.4 %fusion.59 = (f32[768]{0:T(1024)S(1)}, f32[16,768,128]{1,2,0:T(8,128)}) fusion(f32[16,768,128]{1,2,0:T(8,128)S(1)} %copy-done.12, f32[16,128,768]{2,1,0:T(8,128)S(1)} %fusion.81, bf16[16,768,128]{1,2,0:T(8,128)(2,1)S(1)} %bitcast.190, f32[16,128,128]{2,1,0:T(8,128)S(1)} %get-tuple-element.215, f32[16,768]{1,0:T(8,128)S(1)} %get-tuple-element.336), kind=kOutput, calls=%fused_computation.68 | convolution fusion | flops 411565312 | bytes 23120896 | tf_op jit(solution)/shard_map/htd,hde->hte/dot_general | solution.py:41
  159.4 6.6 %copy.79 = f32[768,2048]{1,0:T(8,128)} copy(f32[768,2048]{0,1:T(8,128)} %bitcast.193) | data formatting | bytes 12582912 | tf_op jit(solution)/shard_map/reshape | solution.py:59
  166.0 5.8 %psum.14 = f32[768]{0:T(1024)S(1)} all-reduce(f32[768]{0:T(1024)S(1)} %get-tuple-element.338), channel_id=1, replica_groups=mesh['seq'=8,'head'=4] {'head'}, use_global_device_ids=true, to_apply=%region_7.8 | all-reduce | flops 768 | bytes 6144 | tf_op jit(solution)/shard_map/psum | solution.py:103
  171.8 4.8 %fusion.56 = (f32[2048]{0:T(1024)S(1)}, f32[768]{0:T(1024)S(1)}) fusion(bf16[768,2048]{1,0:T(8,128)(2,1)} %param.19, f32[768,2048]{1,0:T(8,128)} %copy.79, f32[768]{0:T(1024)S(1)} %add_rsqrt_fusion, f32[2048]{0:T(1024)S(1)} %copy-done.13), kind=kLoop, calls=%fused_computation.62 | loop fusion | flops 11007232 | bytes 9459712 | tf_op jit(solution)/shard_map/reduce_sum | solution.py:109
  176.6 6.4 %psum.15 = f32[768]{0:T(1024)S(1)} all-reduce(f32[768]{0:T(1024)S(1)} %get-tuple-element.281), channel_id=1, replica_groups=mesh['seq'=8,'head'=4] {'head'}, use_global_device_ids=true, to_apply=%region_9.10 | all-reduce | flops 768 | bytes 6144 | tf_op jit(solution)/shard_map/psum | solution.py:106
  183.0 5.9 %fusion.68 = (bf16[96,16,8,128]{3,2,1,0:T(8,128)(2,1)S(1)}, bf16[768,2048]{1,0:T(8,128)(2,1)}) fusion(f32[768,2048]{1,0:T(8,128)} %copy.79, bf16[768,2048]{1,0:T(8,128)(2,1)} %param.19, f32[768]{0:T(1024)S(1)} %broadcast_multiply_fusion, f32[2048]{0:T(1024)S(1)} %copy-done.13, f32[768]{0:T(1024)S(1)} %add_rsqrt_fusion), kind=kLoop, calls=%fused_computation.82 | loop fusion | flops 14155776 | bytes 15742976
  198.4 3.4 broadcast.34.clone
  201.8 3.2 broadcast.34.clone2.1
  205.0 3.3 broadcast.34.clone2.2
  208.3 137.7 %while.52 = (s32[]{:T(128)}, f32[16,768,128]{1,2,0:T(8,128)}, f32[16,768,128]{1,2,0:T(8,128)}, f32[16,768,128]{1,2,0:T(8,128)}, bf16[16,768,128]{2,1,0:T(8,128)(...) while((s32[]{:T(128)}, f32[16,768,128]{1,2,0:T(8,128)}, ...), condition=%wide.region_11.12_spmd, body=%wide.region_10.11_spmd.sunk | while | flops 762052608 | bytes 6122609 | solution.py:120
  348.7 3.0 fusion.79
  351.7 8.8 %collective-permute-start.2 = (f32[2048]{0:T(1024)S(1)}, f32[2048]{0:T(1024)S(1)}, u32[]{:S(2)}, u32[]{:S(2)}) collective-permute-start(f32[2048]{0:T(1024)S(1)} %add.110), channel_id=1, source_target_pairs={{0,16},{4,20},{8,24},{12,28},{16,0},{20,4},{24,8},{28,12},{1,17},{... | collective-permute-start | bytes 24584 | tf_op jit(solution)/shard_map/ppermute | solution.py:112
  360.6 3.1 add_convert_fusion
  363.7 4.6 %copy.93 = bf16[768,2048]{1,0:T(8,128)(2,1)} copy(bf16[768,2048]{0,1:T(8,128)(2,1)} %bitcast.194) | data formatting | bytes 6291456
  369.0 10.7 %while.53 = (s32[]{:T(128)}, f32[16,128,128]{2,1,0:T(8,128)S(1)}, s32[]{:T(128)}, f32[8,16]{1,0:T(8,128)S(1)}, f32[8,16,128,128]{3,2,1,0:T(8,128)}, /*index=5*/s32[]{:T(128)}, s32[]{:T(128)}, s32[]{:T(128)}, s32[]{:T(128)}) while((s32[]{:T(128)}, f32[16,128,128]{2,1,0:T(8,128)S(1)}, s32[]{:T(128)}, f32[8,16]{1,0:T(8,128)S(1)}, ...), condition=%wide.region_13.14_spmd, body=%wide.region_12.13_spmd.sunk | while | flops 524294 | bytes 3146075 | solution.py:24
  379.7 3.0 fusion.77
  382.7 3.7 fusion.75
  386.4 5.5 %fusion.58 = bf16[16,768,128]{1,2,0:T(8,128)(2,1)} fusion(f32[16,768,128]{1,2,0:T(8,128)} %get-tuple-element.217, f32[16,128,768]{2,1,0:T(8,128)S(1)} %fusion.77, f32[16,768]{1,0:T(8,128)S(1)} %get-tuple-element.337, bf16[16,768,128]{1,2,0:T(8,128)(2,1)S(1)} %bitcast.187, f32[16,128,128]{2,1,0:T(8,128)S(1)} %get-tuple-element.218), kind=kOutput, calls=%fused_computation.66 | convolution fusion | flops 409993216 | bytes 19972096 | tf_op jit(solution)/shard_map/hse,hde->hsd/dot_general | solution.py:41
  392.0 4.6 %copy.94 = bf16[768,2048]{1,0:T(8,128)(2,1)} copy(bf16[768,2048]{0,1:T(8,128)(2,1)} %bitcast.196) | data formatting | bytes 6291456
  396.6 8.3 %fusion.57 = bf16[16,768,128]{1,2,0:T(8,128)(2,1)} fusion(f32[16,768,128]{1,2,0:T(8,128)} %get-tuple-element.219, f32[16,128,768]{2,1,0:T(8,128)} %fusion.75, f32[16,768]{1,0:T(8,128)S(1)} %get-tuple-element.337, bf16[16,768,128]{1,2,0:T(8,128)(2,1)} %bitcast.181, f32[16,128,128]{2,1,0:T(8,128)S(1)} %get-tuple-element.218), kind=kOutput, calls=%fused_computation.64 | convolution fusion | flops 409993216 | bytes 19972096 | tf_op jit(solution)/shard_map/hsd,hde->hse/dot_general | solution.py:41
  404.9 4.6 %copy.95 = bf16[768,2048]{1,0:T(8,128)(2,1)} copy(bf16[768,2048]{0,1:T(8,128)(2,1)} %bitcast.195) | data formatting | bytes 6291456
  (190 shorter events, 215.9 us)
Async XLA Ops:
  7.2 3.3 copy-start
  7.2 143.0 %all-gather.6.cloned.1.call-start = ((), (), s32[]{:S(2)}) async-start(), calls=%async_computation | async-start | bytes 9437184 | tf_op jit(solution)/shard_map/all_gather | solution.py:15
  10.4 12.1 %copy-start.2 = (bf16[768,2048]{0,1:T(8,128)(2,1)}, bf16[768,2048]{0,1:T(8,128)(2,1)S(1)}, u32[]{:S(2)}) copy-start(bf16[768,2048]{0,1:T(8,128)(2,1)S(1)} %copy.65) | copy-start | bytes 9437188
  17.4 3.0 copy-start.4
  22.5 346.4 %all-gather.8.cloned.1.call-start = ((), (), s32[]{:S(2)}) async-start(), calls=%async_computation.1 | async-start | bytes 9437184 | tf_op jit(solution)/shard_map/all_gather | solution.py:15
  33.3 3.2 copy-start.6
  33.3 3.2 copy-start.14
  150.3 3.1 copy-start.7
  150.3 4.7 %copy-start.12 = (f32[16,768,128]{1,2,0:T(8,128)S(1)}, f32[16,768,128]{1,2,0:T(8,128)}, u32[]{:S(2)}) copy-start(f32[16,768,128]{1,2,0:T(8,128)} %get-tuple-element.214) | copy-start | bytes 18874372
  159.4 12.4 %copy-start.13 = (f32[2048]{0:T(1024)S(1)}, f32[2048]{0:T(1024)}, u32[]{:S(2)}) copy-start(f32[2048]{0:T(1024)} %param.18) | copy-start | bytes 24580
  188.9 5.2 %copy-start.9 = (bf16[96,16,8,128]{3,2,1,0:T(8,128)(2,1)}, bf16[96,16,8,128]{3,2,1,0:T(8,128)(2,1)S(1)}, u32[]{:S(2)}) copy-start(bf16[96,16,8,128]{3,2,1,0:T(8,128)(2,1)S(1)} %get-tuple-element.334) | copy-start | bytes 9437188
  188.9 4.2 copy-start.8
  196.3 149.7 %collective-permute-start = (f32[2048]{0:T(1024)S(1)}, f32[2048]{0:T(1024)S(1)}, u32[]{:S(2)}, u32[]{:S(2)}) collective-permute-start(f32[2048]{0:T(1024)S(1)} %get-tuple-element.280), channel_id=1, source_target_pairs={{0,4},{4,0},{8,12},{12,8},{16,20},{20,16},{24,28},{28,24},{1,5},{5... | collective-permute-start | bytes 24584 | tf_op jit(solution)/shard_map/ppermute | solution.py:112
  346.1 14.5 %copy-start.10 = (bf16[96,16,8,128]{3,2,1,0:T(8,128)(2,1)S(1)}, bf16[96,16,8,128]{3,2,1,0:T(8,128)(2,1)}, u32[]{:S(2)}) copy-start(bf16[96,16,8,128]{3,2,1,0:T(8,128)(2,1)} %copy-done.9) | copy-start | bytes 9437188
  346.1 14.5 %copy-start.11 = (f32[16,768,128]{1,2,0:T(8,128)S(1)}, f32[16,768,128]{1,2,0:T(8,128)}, u32[]{:S(2)}) copy-start(f32[16,768,128]{1,2,0:T(8,128)} %get-tuple-element.216) | copy-start | bytes 18874372
  346.1 5.6 %collective-permute-start.1 = (f32[2048]{0:T(1024)S(1)}, f32[2048]{0:T(1024)S(1)}, u32[]{:S(2)}, u32[]{:S(2)}) collective-permute-start(f32[2048]{0:T(1024)S(1)} %add.109), channel_id=1, source_target_pairs={{0,8},{4,12},{8,0},{12,4},{16,24},{20,28},{24,16},{28,20},{1,9},{5... | collective-permute-start | bytes 24584 | tf_op jit(solution)/shard_map/ppermute | solution.py:112
  351.7 16.6 %collective-permute-start.2 = (f32[2048]{0:T(1024)S(1)}, f32[2048]{0:T(1024)S(1)}, u32[]{:S(2)}, u32[]{:S(2)}) collective-permute-start(f32[2048]{0:T(1024)S(1)} %add.110), channel_id=1, source_target_pairs={{0,16},{4,20},{8,24},{12,28},{16,0},{20,4},{24,8},{28,12},{1,17},{... | collective-permute-start | bytes 24584 | tf_op jit(solution)/shard_map/ppermute | solution.py:112
  379.7 3.0 copy-start.3
  382.7 3.7 copy-start.5
  404.9 4.6 %copy-start.1 = (f32[16,768]{1,0:T(8,128)S(1)}, f32[16,768]{1,0:T(8,128)}, u32[]{:S(2)}) copy-start(f32[16,768]{1,0:T(8,128)} %param.17) | copy-start | bytes 147460
Sparse Core Ops, SparseCore 0:
  22.6 127.5 all-gather.5
  196.5 132.5 all-gather.7
